TPU v7x, 512 devices: a whole 4x4x16 slice. The times are simulated.
512 devices in a mesh: dom: 128 (over z, y, core), src: 4 (over x).
Axes of the slice: x: 4, y: 4, z: 16, core: 2. Of those that a mesh axis runs over, the one named last changes fastest.
Arguments:
- features: bfloat16 [524288, 256], P(('dom', 'src')), may hold values from -6 to 6
- cotangent: bfloat16 [524288, 256], P(('dom', 'src')), may hold values from -6 to 6
- w_self: bfloat16 [256, 256], replicated, may hold values from -0.375 to 0.375
- w_neigh: bfloat16 [256, 256], replicated, may hold values from -0.375 to 0.375
- bias: bfloat16 [256], replicated, may hold values from -3 to 3
- send_rows: int32 [128, 4, 128, 8], P('dom', 'src'), may hold values from -1 to 1023, as said below
- edge_src: int32 [128, 4, 8192], P('dom', 'src'), may hold values from 0 to 2047, as said below
- edge_dst: int32 [128, 4, 8192], P('dom', 'src'), may hold values from 0 to 4095
- tile_count: int32 [128, 4], P('dom', 'src'), may hold values from 16 to 64, as said below
Outputs:
- activations: bfloat16 [524288, 256], P(('dom', 'src'))
- feature_grad: float32 [524288, 256], P(('dom', 'src'))
Inputs may be any that keep to these rules, and one draw needn't show every extreme that they name: `send_rows`: slots of a list are filled from the first one; some list of every owner is full; an account's own part sends it nothing. `edge_src`: every edge refers to a local row or to a filled slot. Edge slots after the first tile_count * 128 are ignored.
All inputs are finite; a program needn't handle non-finite values.
Results may differ from a plain program's by a relative error of at most 0.009.
Values may be sent and summed in bfloat16 or wider, within the bound.
No kernel may reach another device: no remote copies, remote signals or barrier semaphores. Data moves between devices by JAX's collectives and lax.ppermute only.
A program may use at most 64 MiB of HBM per device.

v0:
```python
import jax
import jax.numpy as jnp
from jax import lax
from jax.sharding import PartitionSpec as P


def local(features, cotangent, w_self, w_neigh, bias, send_rows, edge_src, edge_dst, tile_count):
    node_rows = features.shape[0]
    feature_width = features.shape[1]
    peer_total = lax.axis_size("dom")
    senders = send_rows[0, 0]
    capacity = senders.shape[1]
    halo_total = peer_total * capacity
    sources = edge_src[0, 0]
    targets = edge_dst[0, 0]
    edge_total = sources.shape[0]
    part_total = node_rows * lax.axis_size("src")
    active = jnp.arange(edge_total) // 128 < tile_count[0, 0]
    filled = senders >= 0
    zero_half = jnp.zeros((), jnp.bfloat16)
    picked = jnp.where(filled[:, :, None], features[jnp.maximum(senders, 0)], zero_half)
    counts = jnp.zeros((part_total,), jnp.float32).at[targets].add(active.astype(jnp.float32))
    degree_all = lax.psum(counts, "src")
    inverse_all = 1.0 / jnp.maximum(degree_all, 1.0)
    inverse = lax.dynamic_slice_in_dim(inverse_all, lax.axis_index("src") * node_rows, node_rows)
    remote = lax.all_to_all(picked, "dom", split_axis=0, concat_axis=0, tiled=True).reshape(
        halo_total, feature_width
    )
    table = jnp.concatenate([features, remote], axis=0)
    taken = jnp.where(active[:, None], table[sources], zero_half)
    partial_value = (
        jnp.zeros((part_total, feature_width), jnp.float32)
        .at[targets]
        .add(taken.astype(jnp.float32))
    )
    totals = lax.psum_scatter(
        partial_value.astype(jnp.bfloat16), "src", scatter_dimension=0, tiled=True
    ).astype(jnp.float32)
    neighbour_mean = (totals * inverse[:, None]).astype(jnp.bfloat16)
    preact = (
        jnp.dot(features, w_self, preferred_element_type=jnp.float32)
        + jnp.dot(neighbour_mean, w_neigh, preferred_element_type=jnp.float32)
        + bias.astype(jnp.float32)
    )
    sigma = jax.nn.sigmoid(preact)
    outputs = (preact * sigma).astype(jnp.bfloat16)
    slope = sigma * (1.0 + preact * (1.0 - sigma))
    upstream = (cotangent.astype(jnp.float32) * slope).astype(jnp.bfloat16)
    grad_own = jnp.dot(upstream, w_self.T, preferred_element_type=jnp.float32)
    scaled = (
        jnp.dot(upstream, w_neigh.T, preferred_element_type=jnp.float32) * inverse[:, None]
    ).astype(jnp.bfloat16)
    spread = lax.all_gather(scaled, "src", axis=0, tiled=True)
    contrib = jnp.where(active[:, None], spread[targets], zero_half).astype(jnp.float32)
    grad_table = (
        jnp.zeros((node_rows + halo_total, feature_width), jnp.float32).at[sources].add(contrib)
    )
    remote_grad = grad_table[node_rows:]
    local_grad = grad_table[:node_rows]
    returned = lax.all_to_all(
        remote_grad.reshape(peer_total, capacity, feature_width).astype(jnp.bfloat16),
        "dom",
        split_axis=0,
        concat_axis=0,
        tiled=True,
    ).astype(jnp.float32)
    back_rows = jnp.where(filled, senders, node_rows)
    incoming = (
        jnp.zeros((node_rows, feature_width), jnp.float32).at[back_rows].add(returned, mode="drop")
    )
    return (outputs, grad_own + local_grad + incoming)


def solution(mesh):
    placed = (
        P(("dom", "src"), None),
        P(("dom", "src"), None),
        P(),
        P(),
        P(),
        P("dom", "src", None, None),
        P("dom", "src", None),
        P("dom", "src", None),
        P("dom", "src"),
    )
    return jax.shard_map(
        local,
        mesh=mesh,
        in_specs=placed,
        out_specs=(P(("dom", "src"), None), P(("dom", "src"), None)),
        check_vma=False,
    )
```

profile of v0, /device:TPU:33, one launch (start us, length us, event | category | flops | bytes accessed | tf_op | source)
XLA Modules:
  0.0 406.9 jit_solution(14900899894254317384)
XLA Ops:
  7.2 0.8 compare_select_fusion.2
  8.0 0.7 compare_bitcast_fusion
  8.7 0.1 copy.13
  8.8 0.1 reshape.127
  8.9 0.1 copy.12
  9.0 4.6 %gather_fusion = bf16[1024,256]{1,0:T(8,128)(2,1)S(1)} fusion(bf16[1024,256]{1,0:T(8,128)(2,1)} %param.9, s32[1024]{0:T(1024)S(1)} %broadcast_clamp_fusion.2), kind=kCustom, calls=%fused_computation | custom fusion | bytes 1052672 | tf_op jit(solution)/shard_map/gather | solution.py:21
  13.6 1.0 bitcast_select_fusion
  14.6 19.5 %all-to-all-start = ((bf16[128,8,256]{2,1,0:T(8,128)(2,1)}), bf16[128,8,256]{2,1,0:T(8,128)(2,1)S(1)}, u32[]{:S(2)}, u32[]{:S(2)}) async-start(bf16[128,8,256]{2,1,0:T(8,128)(2,1)} %bitcast_select_fusion), calls=%async_computation | async-start | bytes 1048576 | tf_op jit(solution)/shard_map/all_to_all | solution.py:26
  34.9 32.7 %all-to-all-done = bf16[128,8,256]{2,1,0:T(8,128)(2,1)S(1)} async-done(((bf16[128,8,256]{2,1,0:T(8,128)(2,1)}), bf16[128,8,256]{2,1,0:T(8,128)(2,1)S(1)}, u32[]{:S(2)}, u32[]{:S(2)}) %all-to-all-start) | async-done | bytes 524320 | tf_op jit(solution)/shard_map/all_to_all | solution.py:26
  67.7 76.8 %scatter_custom_fusion = f32[4096,256]{1,0:T(8,128)} fusion(s32[8192]{0:T(1024)S(1)} %bitcast.39, pred[8192]{0:T(1024)(128)(4,1)S(1)} %fusion.19, bf16[]{:T(256)} %constant.41.clone.1, f32[]{:T(128)} %constant.14.clone.1, bf16[2048,256]{1,0:T(8,128)(2,1)S(1)} %pad_maximum_fusion, s32[8192]{0:T(1024)S(1)} %broadcast_clamp_fusion.1), kind=kCustom, calls=%fused_computation.9 | custom fusion | flops 6291456 | bytes 5283846 | tf_op jit(solution)/shard_map/scatter-add | solution.py:34
  144.6 3.8 convert_element_type.41
  148.4 43.2 %scatter_custom_fusion.1 = f32[4096]{0:T(1024)S(1)} fusion(s32[8192]{0:T(1024)S(1)} %bitcast.40, f32[8192]{0:T(1024)S(1)} %fusion.25, f32[]{:T(128)} %constant.14.clone.1), kind=kCustom, calls=%fused_computation.50 | custom fusion | flops 8192 | bytes 16388 | tf_op jit(solution)/shard_map/scatter-add | solution.py:22
  191.7 13.2 %psum.7 = f32[4096]{0:T(1024)S(1)} all-reduce(f32[4096]{0:T(1024)S(1)} %scatter_custom_fusion.1), channel_id=1, replica_groups=mesh['dom'=128,'src'=4] {'src'}, use_global_device_ids=true, to_apply=%region_3.4 | all-reduce | flops 4096 | bytes 32768 | tf_op jit(solution)/shard_map/psum | solution.py:23
  204.8 0.3 fusion.29
  205.2 2.6 multiply_convert_fusion
  207.8 1.1 fusion.12
  208.9 31.2 %all-gather.2.cloned.1.call-done = bf16[4096,256]{1,0:T(8,128)(2,1)} async-done(((bf16[1024,256]{1,0:T(8,128)(2,1)}), bf16[4096,256]{1,0:T(8,128)(2,1)}) %all-gather.2.cloned.1.call-update) | async-done | bytes 2097168 | tf_op jit(solution)/shard_map/all_gather | solution.py:53
  240.1 100.4 %scatter_custom_fusion.2 = f32[2048,256]{1,0:T(8,128)S(1)} fusion(s32[8192]{0:T(1024)S(1)} %bitcast.38, pred[8192]{0:T(1024)(128)(4,1)S(1)} %fusion.19, bf16[]{:T(256)} %constant.41.clone.1, f32[]{:T(128)} %constant.14.clone.1, bf16[4096,256]{1,0:T(8,128)(2,1)} %all-gather.2.cloned.1.call-done, s32[8192]{0:T(1024)S(1)} %broadcast_clamp_fusion), kind=kCustom, calls=%fused_computation.7 | custom fusion | flops 6291456 | bytes 4235270 | tf_op jit(solution)/shard_map/scatter-add | solution.py:56
  340.5 0.8 fusion.16
  341.4 16.8 %all-to-all-start.1 = ((bf16[128,8,256]{2,1,0:T(8,128)(2,1)}), bf16[128,8,256]{2,1,0:T(8,128)(2,1)S(1)}, u32[]{:S(2)}, u32[]{:S(2)}) async-start(bf16[128,8,256]{2,1,0:T(8,128)(2,1)} %fusion.16), calls=%async_computation.2 | async-start | bytes 1048576 | tf_op jit(solution)/shard_map/all_to_all | solution.py:60
  358.2 0.1 copy.14
  358.4 1.3 convolution_add_fusion
  359.7 32.1 %all-to-all-done.1 = bf16[128,8,256]{2,1,0:T(8,128)(2,1)S(1)} async-done(((bf16[128,8,256]{2,1,0:T(8,128)(2,1)}), bf16[128,8,256]{2,1,0:T(8,128)(2,1)S(1)}, u32[]{:S(2)}, u32[]{:S(2)}) %all-to-all-start.1) | async-done | bytes 524320 | tf_op jit(solution)/shard_map/all_to_all | solution.py:60
  391.8 8.3 %scatter_custom_fusion.3 = f32[1024,256]{1,0:T(8,128)} fusion(f32[1024,256]{1,0:T(8,128)} %convolution_add_fusion, s32[1024]{0:T(1024)S(1)} %reshape.175, bf16[128,8,256]{2,1,0:T(8,128)(2,1)S(1)} %all-to-all-done.1), kind=kCustom, calls=%fused_computation.25 | custom fusion | flops 524288 | bytes 1572864 | tf_op jit(solution)/shard_map/scatter-add | solution.py:69
  (30 shorter events, 0.5 us)
Async XLA Ops:
  7.2 198.0 %copy-start = (bf16[256,256]{1,0:T(8,128)(2,1)S(1)}, bf16[256,256]{1,0:T(8,128)(2,1)}, u32[]{:S(2)}) copy-start(bf16[256,256]{1,0:T(8,128)(2,1)} %param.12) | copy-start | bytes 393220
  7.2 60.5 %copy-start.1 = (bf16[1024,256]{1,0:T(8,128)(2,1)S(1)}, bf16[1024,256]{1,0:T(8,128)(2,1)}, u32[]{:S(2)}) copy-start(bf16[1024,256]{1,0:T(8,128)(2,1)} %param.9) | copy-start | bytes 1572868
  7.2 27.6 %copy-start.3 = (s32[1,1,8192]{2,1,0:T(1,128)S(1)}, s32[1,1,8192]{2,1,0:T(1,128)}, u32[]{:S(2)}) copy-start(s32[1,1,8192]{2,1,0:T(1,128)} %param.15) | copy-start | bytes 98308
  7.2 27.6 %copy-start.4 = (s32[1,1,8192]{2,1,0:T(1,128)S(1)}, s32[1,1,8192]{2,1,0:T(1,128)}, u32[]{:S(2)}) copy-start(s32[1,1,8192]{2,1,0:T(1,128)} %param.16) | copy-start | bytes 98308
  14.6 53.1 %all-to-all-start = ((bf16[128,8,256]{2,1,0:T(8,128)(2,1)}), bf16[128,8,256]{2,1,0:T(8,128)(2,1)S(1)}, u32[]{:S(2)}, u32[]{:S(2)}) async-start(bf16[128,8,256]{2,1,0:T(8,128)(2,1)} %bitcast_select_fusion), calls=%async_computation | async-start | bytes 1048576 | tf_op jit(solution)/shard_map/all_to_all | solution.py:26
  34.1 171.1 %reduce-scatter.2.cloned.1.call-start = ((), (), s32[]{:S(2)}) async-start(), calls=%async_computation.3 | async-start | bytes 2621440 | tf_op jit(solution)/shard_map/reduce_scatter | solution.py:36
  144.6 47.1 %copy-start.6 = (bf16[256]{0:T(256)(128)(2,1)S(1)}, bf16[256]{0:T(256)(128)(2,1)}, u32[]{:S(2)}) copy-start(bf16[256]{0:T(256)(128)(2,1)} %param.13) | copy-start | bytes 1540
  144.6 60.3 %copy-start.2 = (bf16[256,256]{1,0:T(8,128)(2,1)S(1)}, bf16[256,256]{1,0:T(8,128)(2,1)}, u32[]{:S(2)}) copy-start(bf16[256,256]{1,0:T(8,128)(2,1)} %param.11) | copy-start | bytes 393220
  144.6 60.6 %copy-start.5 = (bf16[1024,256]{1,0:T(8,128)(2,1)S(1)}, bf16[1024,256]{1,0:T(8,128)(2,1)}, u32[]{:S(2)}) copy-start(bf16[1024,256]{1,0:T(8,128)(2,1)} %param.10) | copy-start | bytes 1572868
  148.4 91.8 %all-gather.2.cloned.1.call-start = ((), (), s32[]{:S(2)}) async-start(), calls=%async_computation.4 | async-start | bytes 2621440 | tf_op jit(solution)/shard_map/all_gather | solution.py:53
  341.4 50.4 %all-to-all-start.1 = ((bf16[128,8,256]{2,1,0:T(8,128)(2,1)}), bf16[128,8,256]{2,1,0:T(8,128)(2,1)S(1)}, u32[]{:S(2)}, u32[]{:S(2)}) async-start(bf16[128,8,256]{2,1,0:T(8,128)(2,1)} %fusion.16), calls=%async_computation.2 | async-start | bytes 1048576 | tf_op jit(solution)/shard_map/all_to_all | solution.py:60
Sparse Core Ops, SparseCore 0:
  148.5 28.3 reduce-scatter.1
  209.0 31.0 all-gather.1
where the time goes:
time: 408 us; the launch traced here: 407 us
  other arithmetic  235 us (58%)
  waiting for transfers between devices  96.1 us (24%)
  starting transfers between devices  36.4 us (9%)
  between operations  14.9 us (4%)
  blocking collectives  13.2 us (3%)
  local copies, waits for them, and re-layouts  5.95 us (1%)
  matrix products  5.3 us (1%)
    scatter-add x1, other arithmetic, local(): jnp.zeros((node_rows + halo_total, feature_width), jnp.float32).at[sources]  100 us
    scatter-add x1, other arithmetic, local(): partial_value = jnp.zeros((part_total, feature_width), jnp.float32).at[ta...  76.8 us
    scatter-add x1, other arithmetic, local(): jnp.zeros((part_total,), jnp.float32).at[targets]  43.2 us
    all_to_all x1, waiting for transfers between devices, local(): lax.all_to_all(picked, 'dom', split_axis=0, concat_axis=0, tiled=True)  32.7 us
    all_to_all x1, waiting for transfers between devices, local(): lax.all_to_all(remote_grad.reshape(peer_total, capacity, feature_width).a...  32.1 us
    all_gather x1, waiting for transfers between devices, local(): spread = lax.all_gather(scaled, 'src', axis=0, tiled=True)  31.2 us
    all_to_all x1, starting transfers between devices, local(): lax.all_to_all(picked, 'dom', split_axis=0, concat_axis=0, tiled=True)  19.5 us
    all_to_all x1, starting transfers between devices, local(): lax.all_to_all(remote_grad.reshape(peer_total, capacity, feature_width).a...  16.8 us
  transfers between devices with their start and end apart: 4, of which 3 were waited for; matrix products, arithmetic and copies ran while one was open for 11% of the time, Pallas kernels for 0%

commit v1 on v0

--- a/solution.py
+++ b/solution.py
@@ -50,7 +50,23 @@
     scaled = (
         jnp.dot(upstream, w_neigh.T, preferred_element_type=jnp.float32) * inverse[:, None]
     ).astype(jnp.bfloat16)
-    spread = lax.all_gather(scaled, "src", axis=0, tiled=True)
+    size, mine, rows = (lax.axis_size("src"), lax.axis_index("src"), scaled.shape[0])
+    forward = [(i, (i + 1) % size) for i in range(size)]
+    backward = [(i, (i - 1) % size) for i in range(size)]
+    spread = jnp.zeros((*scaled.shape[:0], size * rows, *scaled.shape[0 + 1 :]), scaled.dtype)
+    spread = lax.dynamic_update_slice_in_dim(spread, scaled, mine * rows, axis=0)
+    from_left = from_right = scaled
+    halfway = size // 2
+    for step in range(1, halfway + 1):
+        from_left = lax.ppermute(from_left, "src", forward)
+        spread = lax.dynamic_update_slice_in_dim(
+            spread, from_left, (mine - step) % size * rows, axis=0
+        )
+        if step < size - halfway:
+            from_right = lax.ppermute(from_right, "src", backward)
+            spread = lax.dynamic_update_slice_in_dim(
+                spread, from_right, (mine + step) % size * rows, axis=0
+            )
     contrib = jnp.where(active[:, None], spread[targets], zero_half).astype(jnp.float32)
     grad_table = (
         jnp.zeros((node_rows + halo_total, feature_width), jnp.float32).at[sources].add(contrib)

time: 408 us -> 373 us (0.914)
  other arithmetic: 235 us -> 211 us
  waiting for transfers between devices: 96.1 us -> 79.4 us
  local copies, waits for them, and re-layouts: 5.95 us -> 10.7 us
    all_gather x1 -> x0, waiting for transfers between devices: 31.2 us -> none  [local(): spread = lax.all_gather(scaled, 'src', axis=0, tiled=True)]
    scatter-add x1, other arithmetic: 100 us -> 76.1 us  [local(): jnp.zeros((node_rows + halo_total, feature_width), jnp.float32).at[sources]]
    ppermute x0 -> x3, waiting for transfers between devices: none -> 14.5 us  [the longest x2 14.5 us: local(): from_left = lax.ppermute(from_left, 'src', forward)]
    ppermute x0 -> x3, starting transfers between devices: none -> 8.59 us  [the longest x1 4.57 us: local(): from_right = lax.ppermute(from_right, 'src', backward)]
    all_to_all x1, starting transfers between devices: 16.8 us -> 11.1 us  [local(): lax.all_to_all(remote_grad.reshape(peer_total, capacity, feature_width).a...]
  transfers between devices with their start and end apart: 4 -> 6, of which waited for: 3 -> 4; matrix products, arithmetic and copies ran while one was open for 11% -> 13% of each run, Pallas kernels for 0% -> 0%
where the time goes in v1:
time: 373 us
  other arithmetic  211 us (57%)
  waiting for transfers between devices  79.4 us (21%)
  starting transfers between devices  39.2 us (11%)
  between operations  15 us (4%)
  blocking collectives  13.1 us (4%)
  local copies, waits for them, and re-layouts  10.7 us (3%)
  matrix products  4.51 us (1%)
    scatter-add x1, other arithmetic, local(): partial_value = jnp.zeros((part_total, feature_width), jnp.float32).at[ta...  76.8 us
    scatter-add x1, other arithmetic, local(): jnp.zeros((node_rows + halo_total, feature_width), jnp.float32).at[sources]  76.1 us
    scatter-add x1, other arithmetic, local(): jnp.zeros((part_total,), jnp.float32).at[targets]  43.2 us
    all_to_all x1, waiting for transfers between devices, local(): lax.all_to_all(picked, 'dom', split_axis=0, concat_axis=0, tiled=True)  32.7 us
    all_to_all x1, waiting for transfers between devices, local(): lax.all_to_all(remote_grad.reshape(peer_total, capacity, feature_width).a...  32.1 us
    all_to_all x1, starting transfers between devices, local(): lax.all_to_all(picked, 'dom', split_axis=0, concat_axis=0, tiled=True)  19.5 us
    ppermute x2, waiting for transfers between devices, local(): from_left = lax.ppermute(from_left, 'src', forward)  14.5 us
    psum x1, blocking collectives, local(): degree_all = lax.psum(counts, 'src')  13.1 us
  transfers between devices with their start and end apart: 6, of which 4 were waited for; matrix products, arithmetic and copies ran while one was open for 13% of the time, Pallas kernels for 0%

profile of v1, /device:TPU:33, one launch (start us, length us, event | category | flops | bytes accessed | tf_op | source)
XLA Modules:
  0.0 372.7 jit_solution(11823199164143056443)
XLA Ops:
  7.2 0.7 compare_select_fusion.2
  8.9 4.6 %gather_fusion = bf16[1024,256]{1,0:T(8,128)(2,1)S(1)} fusion(bf16[1024,256]{1,0:T(8,128)(2,1)} %param.9, s32[1024]{0:T(1024)S(1)} %broadcast_clamp_fusion.2), kind=kCustom, calls=%fused_computation | custom fusion | bytes 1052672 | tf_op jit(solution)/shard_map/gather | solution.py:21
  13.5 1.0 bitcast_select_fusion
  14.5 19.5 %all-to-all-start = ((bf16[128,8,256]{2,1,0:T(8,128)(2,1)}), bf16[128,8,256]{2,1,0:T(8,128)(2,1)S(1)}, u32[]{:S(2)}, u32[]{:S(2)}) async-start(bf16[128,8,256]{2,1,0:T(8,128)(2,1)} %bitcast_select_fusion), calls=%async_computation | async-start | bytes 1048576 | tf_op jit(solution)/shard_map/all_to_all | solution.py:26
  34.9 32.7 %all-to-all-done = bf16[128,8,256]{2,1,0:T(8,128)(2,1)S(1)} async-done(((bf16[128,8,256]{2,1,0:T(8,128)(2,1)}), bf16[128,8,256]{2,1,0:T(8,128)(2,1)S(1)}, u32[]{:S(2)}, u32[]{:S(2)}) %all-to-all-start) | async-done | bytes 524320 | tf_op jit(solution)/shard_map/all_to_all | solution.py:26
  67.7 76.8 %scatter_custom_fusion = f32[4096,256]{1,0:T(8,128)} fusion(s32[8192]{0:T(1024)S(1)} %bitcast.39, pred[8192]{0:T(1024)(128)(4,1)S(1)} %fusion.19, bf16[]{:T(256)} %constant.64.clone.1, f32[]{:T(128)} %constant.57.clone.1, bf16[2048,256]{1,0:T(8,128)(2,1)S(1)} %pad_maximum_fusion, s32[8192]{0:T(1024)S(1)} %broadcast_clamp_fusion.1), kind=kCustom, calls=%fused_computation.9 | custom fusion | flops 6291456 | bytes 5283846 | tf_op jit(solution)/shard_map/scatter-add | solution.py:34
  144.5 3.7 convert_element_type.41
  148.3 43.2 %scatter_custom_fusion.1 = f32[4096]{0:T(1024)S(1)} fusion(s32[8192]{0:T(1024)S(1)} %bitcast.40, f32[8192]{0:T(1024)S(1)} %fusion.25, f32[]{:T(128)} %constant.57.clone.1), kind=kCustom, calls=%fused_computation.50 | custom fusion | flops 8192 | bytes 16388 | tf_op jit(solution)/shard_map/scatter-add | solution.py:22
  191.5 13.1 %psum.7 = f32[4096]{0:T(1024)S(1)} all-reduce(f32[4096]{0:T(1024)S(1)} %scatter_custom_fusion.1), channel_id=1, replica_groups=mesh['dom'=128,'src'=4] {'src'}, use_global_device_ids=true, to_apply=%region_3.4 | all-reduce | flops 4096 | bytes 32768 | tf_op jit(solution)/shard_map/psum | solution.py:23
  205.0 2.6 multiply_convert_fusion
  208.1 1.9 collective-permute-start
  210.0 4.6 %collective-permute-start.1 = (bf16[1024,256]{1,0:T(8,128)(2,1)S(1)}, bf16[1024,256]{1,0:T(8,128)(2,1)}, u32[]{:S(2)}, u32[]{:S(2)}) collective-permute-start(bf16[1024,256]{1,0:T(8,128)(2,1)S(1)} %get-tuple-element.7), channel_id=1, source_target_pairs={{0,3},{1,0},{2,1},{3,2},{4,7},{5,4},{6,5},{7,6},{8,11},{9,8},{10,9... | collective-permute-start | bytes 1572872 | tf_op jit(solution)/shard_map/ppermute | solution.py:66
  214.6 6.5 %collective-permute-done = bf16[1024,256]{1,0:T(8,128)(2,1)} collective-permute-done((bf16[1024,256]{1,0:T(8,128)(2,1)S(1)}, bf16[1024,256]{1,0:T(8,128)(2,1)}, u32[]{:S(2)}, u32[]{:S(2)}) %collective-permute-start) | collective-permute-done | bytes 524320 | tf_op jit(solution)/shard_map/ppermute | solution.py:61
  221.1 2.1 collective-permute-start.2
  223.3 1.1 constant_dynamic-update-slice_fusion.2
  224.4 1.1 constant_dynamic-update-slice_fusion.1
  225.5 8.0 %collective-permute-done.2 = bf16[1024,256]{1,0:T(8,128)(2,1)} collective-permute-done((bf16[1024,256]{1,0:T(8,128)(2,1)}, bf16[1024,256]{1,0:T(8,128)(2,1)}, u32[]{:S(2)}, u32[]{:S(2)}) %collective-permute-start.2) | collective-permute-done | bytes 524320 | tf_op jit(solution)/shard_map/ppermute | solution.py:61
  233.5 1.1 constant_dynamic-update-slice_fusion
  234.5 76.1 %scatter_custom_fusion.2 = f32[2048,256]{1,0:T(8,128)} fusion(s32[8192]{0:T(1024)S(1)} %bitcast.38, pred[8192]{0:T(1024)(128)(4,1)S(1)} %fusion.19, bf16[]{:T(256)} %constant.64.clone.1, f32[]{:T(128)} %constant.57.clone.1, bf16[4096,256]{1,0:T(8,128)(2,1)S(1)} %constant_dynamic-update-slice_fusion, s32[8192]{0:T(1024)S(1)} %broadcast_clamp_fusion), kind=kCustom, calls=%fused_computation.7 | custom fusion | flops 6291456 | bytes 4235270 | tf_op jit(solution)/shard_map/scatter-add | solution.py:72
  310.6 2.2 fusion.16
  312.9 11.1 %all-to-all-start.1 = ((bf16[128,8,256]{2,1,0:T(8,128)(2,1)}), bf16[128,8,256]{2,1,0:T(8,128)(2,1)S(1)}, u32[]{:S(2)}, u32[]{:S(2)}) async-start(bf16[128,8,256]{2,1,0:T(8,128)(2,1)} %fusion.16), calls=%async_computation.2 | async-start | bytes 1048576 | tf_op jit(solution)/shard_map/all_to_all | solution.py:76
  324.2 1.3 slice_add_fusion
  325.5 32.1 %all-to-all-done.1 = bf16[128,8,256]{2,1,0:T(8,128)(2,1)S(1)} async-done(((bf16[128,8,256]{2,1,0:T(8,128)(2,1)}), bf16[128,8,256]{2,1,0:T(8,128)(2,1)S(1)}, u32[]{:S(2)}, u32[]{:S(2)}) %all-to-all-start.1) | async-done | bytes 524320 | tf_op jit(solution)/shard_map/all_to_all | solution.py:76
  357.6 8.3 %scatter_custom_fusion.3 = f32[1024,256]{1,0:T(8,128)} fusion(f32[1024,256]{1,0:T(8,128)} %slice_add_fusion, s32[1024]{0:T(1024)S(1)} %reshape.175, bf16[128,8,256]{2,1,0:T(8,128)(2,1)S(1)} %all-to-all-done.1), kind=kCustom, calls=%fused_computation.25 | custom fusion | flops 524288 | bytes 1572864 | tf_op jit(solution)/shard_map/scatter-add | solution.py:85
  (39 shorter events, 2.3 us)
Async XLA Ops:
  7.2 197.9 %copy-start = (bf16[256,256]{1,0:T(8,128)(2,1)S(1)}, bf16[256,256]{1,0:T(8,128)(2,1)}, u32[]{:S(2)}) copy-start(bf16[256,256]{1,0:T(8,128)(2,1)} %param.12) | copy-start | bytes 393220
  13.5 21.2 %copy-start.4 = (s32[1,1,8192]{2,1,0:T(1,128)S(1)}, s32[1,1,8192]{2,1,0:T(1,128)}, u32[]{:S(2)}) copy-start(s32[1,1,8192]{2,1,0:T(1,128)} %param.15) | copy-start | bytes 98308
  13.5 21.3 %copy-start.5 = (s32[1,1,8192]{2,1,0:T(1,128)S(1)}, s32[1,1,8192]{2,1,0:T(1,128)}, u32[]{:S(2)}) copy-start(s32[1,1,8192]{2,1,0:T(1,128)} %param.16) | copy-start | bytes 98308
  13.5 54.1 %copy-start.1 = (bf16[1024,256]{1,0:T(8,128)(2,1)S(1)}, bf16[1024,256]{1,0:T(8,128)(2,1)}, u32[]{:S(2)}) copy-start(bf16[1024,256]{1,0:T(8,128)(2,1)} %param.9) | copy-start | bytes 1572868
  14.5 53.1 %all-to-all-start = ((bf16[128,8,256]{2,1,0:T(8,128)(2,1)}), bf16[128,8,256]{2,1,0:T(8,128)(2,1)S(1)}, u32[]{:S(2)}, u32[]{:S(2)}) async-start(bf16[128,8,256]{2,1,0:T(8,128)(2,1)} %bitcast_select_fusion), calls=%async_computation | async-start | bytes 1048576 | tf_op jit(solution)/shard_map/all_to_all | solution.py:26
  34.0 171.0 %reduce-scatter.2.cloned.1.call-start = ((), (), s32[]{:S(2)}) async-start(), calls=%async_computation.3 | async-start | bytes 2621440 | tf_op jit(solution)/shard_map/reduce_scatter | solution.py:36
  148.2 43.3 %copy-start.7 = (bf16[256]{0:T(256)(128)(2,1)S(1)}, bf16[256]{0:T(256)(128)(2,1)}, u32[]{:S(2)}) copy-start(bf16[256]{0:T(256)(128)(2,1)} %param.13) | copy-start | bytes 1540
  148.2 56.4 %copy-start.3 = (bf16[256,256]{1,0:T(8,128)(2,1)S(1)}, bf16[256,256]{1,0:T(8,128)(2,1)}, u32[]{:S(2)}) copy-start(bf16[256,256]{1,0:T(8,128)(2,1)} %param.11) | copy-start | bytes 393220
  148.3 56.8 %copy-start.6 = (bf16[1024,256]{1,0:T(8,128)(2,1)S(1)}, bf16[1024,256]{1,0:T(8,128)(2,1)}, u32[]{:S(2)}) copy-start(bf16[1024,256]{1,0:T(8,128)(2,1)} %param.10) | copy-start | bytes 1572868
  208.1 13.0 %collective-permute-start = (bf16[1024,256]{1,0:T(8,128)(2,1)S(1)}, bf16[1024,256]{1,0:T(8,128)(2,1)}, u32[]{:S(2)}, u32[]{:S(2)}) collective-permute-start(bf16[1024,256]{1,0:T(8,128)(2,1)S(1)} %get-tuple-element.7), channel_id=1, source_target_pairs={{0,1},{1,2},{2,3},{3,0},{4,5},{5,6},{6,7},{7,4},{8,9},{9,10},{10,1... | collective-permute-start | bytes 1572872 | tf_op jit(solution)/shard_map/ppermute | solution.py:61
  210.0 14.4 %collective-permute-start.1 = (bf16[1024,256]{1,0:T(8,128)(2,1)S(1)}, bf16[1024,256]{1,0:T(8,128)(2,1)}, u32[]{:S(2)}, u32[]{:S(2)}) collective-permute-start(bf16[1024,256]{1,0:T(8,128)(2,1)S(1)} %get-tuple-element.7), channel_id=1, source_target_pairs={{0,3},{1,0},{2,1},{3,2},{4,7},{5,4},{6,5},{7,6},{8,11},{9,8},{10,9... | collective-permute-start | bytes 1572872 | tf_op jit(solution)/shard_map/ppermute | solution.py:66
  221.1 12.3 %collective-permute-start.2 = (bf16[1024,256]{1,0:T(8,128)(2,1)}, bf16[1024,256]{1,0:T(8,128)(2,1)}, u32[]{:S(2)}, u32[]{:S(2)}) collective-permute-start(bf16[1024,256]{1,0:T(8,128)(2,1)} %collective-permute-done), channel_id=1, source_target_pairs={{0,1},{1,2},{2,3},{3,0},{4,5},{5,6},{6,7},{7,4},{8,9},{9,10},{10,1... | collective-permute-start | bytes 1572872 | tf_op jit(solution)/shard_map/ppermute | solution.py:61
  310.6 13.5 %copy-start.2 = (f32[2048,256]{1,0:T(8,128)S(1)}, f32[2048,256]{1,0:T(8,128)}, u32[]{:S(2)}) copy-start(f32[2048,256]{1,0:T(8,128)} %scatter_custom_fusion.2) | copy-start | bytes 6291460
  312.9 44.7 %all-to-all-start.1 = ((bf16[128,8,256]{2,1,0:T(8,128)(2,1)}), bf16[128,8,256]{2,1,0:T(8,128)(2,1)S(1)}, u32[]{:S(2)}, u32[]{:S(2)}) async-start(bf16[128,8,256]{2,1,0:T(8,128)(2,1)} %fusion.16), calls=%async_computation.2 | async-start | bytes 1048576 | tf_op jit(solution)/shard_map/all_to_all | solution.py:76
Sparse Core Ops, SparseCore 0:
  148.4 28.3 reduce-scatter.1
